TPU v7x, 32 devices: a whole 2x2x4 slice. The times are simulated.
32 devices in a mesh: wide: 8 (over z, x), narrow: 4 (over y, core).
Axes of the slice: x: 2, y: 2, z: 4, core: 2. Of those that a mesh axis runs over, the one named last changes fastest.
Arguments:
- flow_field: bfloat16 [64, 64, 16, 512], P('wide', 'narrow'), may hold values from -48 to 48
- fluid_mask: int32 [64, 64, 16], P('wide', 'narrow'), may hold values 0 or 1
- conv_weight: float32 [27, 512], replicated, may hold values from -1 to 1
- latents: bfloat16 [1024, 512], replicated, may hold values from -6 to 6
- w_query1: bfloat16 [512, 512], replicated, may hold values from -0.25 to 0.25
- w_key1: bfloat16 [512, 512], replicated, may hold values from -0.25 to 0.25
- w_value1: bfloat16 [512, 512], replicated, may hold values from -0.25 to 0.25
- w_out1: bfloat16 [512, 512], replicated, may hold values from -0.25 to 0.25
- w_query2: bfloat16 [512, 512], replicated, may hold values from -0.25 to 0.25
- w_key2: bfloat16 [512, 512], replicated, may hold values from -0.25 to 0.25
- w_value2: bfloat16 [512, 512], replicated, may hold values from -0.25 to 0.25
- w_out2: bfloat16 [512, 512], replicated, may hold values from -0.25 to 0.25
Outputs:
- updated_field: float32 [64, 64, 16, 512], P('wide', 'narrow')
All inputs are finite; a program needn't handle non-finite values. No bound on the sum of `fluid_mask` on one device may be relied on, other than what follows from the above.
Results may differ from a plain program's by a relative error of at most 0.035.
The roundings to bfloat16 on the way count: a program that leaves them out, or rounds other values in their place, can miss the bound.
Values may be sent and summed in bfloat16 or wider, within the bound.
No kernel may reach another device: no remote copies, remote signals or barrier semaphores. Data moves between devices by JAX's collectives and lax.ppermute only.
A program may use at most 192 MiB of HBM per device.

v0:
```python
import math
import jax
import jax.numpy as jnp
from jax import lax
from jax.sharding import PartitionSpec as P

HEADS = 8


def padded_2(cells, sides, width):
    for axis, dim in sides:
        count = lax.axis_size(axis)
        ends = count - 1
        head = lax.slice_in_dim(cells, 0, width, axis=dim)
        tail = lax.slice_in_dim(cells, cells.shape[dim] - width, cells.shape[dim], axis=dim)
        cells = jnp.concatenate(
            [
                lax.ppermute(tail, axis, [(i, (i + 1) % count) for i in range(ends)]),
                cells,
                lax.ppermute(head, axis, [((i + 1) % count, i) for i in range(ends)]),
            ],
            axis=dim,
        )
    return cells


def head_block(matrix, head_index, head_size):
    return matrix[:, head_index * head_size : (head_index + 1) * head_size]


def pair_scores(queries, key_rows, head_size):
    factor = 1.8 / math.sqrt(head_size)
    return factor * lax.dot_general(
        queries, key_rows, (((1,), (1,)), ((), ())), preferred_element_type=jnp.float32
    )


def project(row_block, weight):
    return jnp.dot(row_block, weight, preferred_element_type=jnp.float32).astype(jnp.bfloat16)


def exact_dot(weights, values_block):
    return jnp.dot(
        weights, values_block, precision=lax.Precision.HIGHEST, preferred_element_type=jnp.float32
    )


def update_state(summed, totals, state_rows, w_out1, head_count):
    row_count, model_width = summed.shape
    shaped = summed.reshape(row_count, head_count, model_width // head_count) / totals[:, :, None]
    read_rows = shaped.reshape(row_count, model_width).astype(jnp.bfloat16)
    updated = state_rows.astype(jnp.float32) + jnp.dot(
        read_rows, w_out1, preferred_element_type=jnp.float32
    )
    return updated.astype(jnp.bfloat16)


def per_device(
    flow_field,
    fluid_mask,
    conv_weight,
    latents,
    w_query1,
    w_key1,
    w_value1,
    w_out1,
    w_query2,
    w_key2,
    w_value2,
    w_out2,
):
    size_x, size_y, size_z, model_width = flow_field.shape
    head_count = HEADS
    head_size = model_width // head_count
    latent_count = latents.shape[0]
    masked = flow_field * fluid_mask[:, :, :, None].astype(jnp.bfloat16)
    padded = padded_2(masked, (("wide", 0), ("narrow", 1)), 1)
    padded = jnp.pad(padded, ((0, 0), (0, 0), (1, 1), (0, 0)))
    stencil = masked.astype(jnp.float32)
    for offset_x in range(3):
        for offset_y in range(3):
            for offset_z in range(3):
                window = padded[
                    offset_x : offset_x + size_x,
                    offset_y : offset_y + size_y,
                    offset_z : offset_z + size_z,
                ]
                stencil = (
                    stencil
                    + window.astype(jnp.float32)
                    * conv_weight[9 * offset_x + 3 * offset_y + offset_z]
                )
    cell_count = size_x * size_y * size_z
    mixed_cells = stencil.astype(jnp.bfloat16).reshape(cell_count, model_width)
    flat_masked = masked.reshape(cell_count, model_width)
    keys1 = project(mixed_cells, w_key1)
    values1 = project(mixed_cells, w_value1)
    values_wide = values1.astype(jnp.float32)
    queries1 = project(latents, w_query1)
    device_count = lax.axis_size("wide") * lax.axis_size("narrow")
    sums_list = []
    totals_list = []
    tops_list = []
    for head_index in range(head_count):
        scores = pair_scores(
            head_block(queries1, head_index, head_size),
            head_block(keys1, head_index, head_size),
            head_size,
        )
        own_top = jnp.max(scores, axis=1, keepdims=True)
        weights = jnp.exp(scores - own_top)
        tops_list.append(own_top[:, 0])
        totals_list.append(jnp.sum(weights, axis=1))
        sums_list.append(exact_dot(weights, head_block(values_wide, head_index, head_size)))
    summed1 = jnp.concatenate(sums_list, axis=1)[None]
    totals1 = jnp.stack(totals_list, axis=1)[None]
    tops1 = jnp.stack(tops_list, axis=1)[None]
    part_sums, part_totals, part_tops = (
        lax.all_to_all(summed1, ("wide", "narrow"), split_axis=1, concat_axis=0, tiled=True),
        lax.all_to_all(totals1, ("wide", "narrow"), split_axis=1, concat_axis=0, tiled=True),
        lax.all_to_all(tops1, ("wide", "narrow"), split_axis=1, concat_axis=0, tiled=True),
    )
    row_count = latent_count // device_count
    largest = jnp.max(part_tops, axis=0, keepdims=True)
    factors = jnp.exp(part_tops - largest)
    totals = jnp.sum(factors * part_totals, axis=0)
    shaped = (
        part_sums.reshape(device_count, row_count, head_count, head_size) * factors[:, :, :, None]
    )
    summed = jnp.sum(shaped, axis=0).reshape(row_count, model_width)
    start = (
        lax.axis_index("wide") * lax.axis_size("narrow") + lax.axis_index("narrow")
    ) * row_count
    own_latents = lax.dynamic_slice_in_dim(latents, start, row_count, 0)
    own_state = update_state(summed, totals, own_latents, w_out1, head_count)
    latent_state = lax.all_gather(own_state, ("wide", "narrow"), axis=0, tiled=True)
    keys2 = project(latent_state, w_key2)
    values2 = project(latent_state, w_value2)
    queries2 = project(mixed_cells, w_query2)
    read_heads = []
    for head_index in range(head_count):
        scores = pair_scores(
            head_block(queries2, head_index, head_size),
            head_block(keys2, head_index, head_size),
            head_size,
        )
        top2 = jnp.max(scores, axis=1, keepdims=True)
        weights = jnp.exp(scores - top2)
        totals = jnp.sum(weights, axis=1, keepdims=True)
        summed = jnp.dot(
            weights.astype(jnp.bfloat16),
            head_block(values2, head_index, head_size),
            preferred_element_type=jnp.float32,
        )
        read_heads.append(summed / totals)
    read2 = jnp.concatenate(read_heads, axis=1).astype(jnp.bfloat16)
    result = flat_masked.astype(jnp.float32) + jnp.dot(
        read2, w_out2, preferred_element_type=jnp.float32
    )
    return result.reshape(size_x, size_y, size_z, model_width)


def solution(mesh):
    return jax.shard_map(
        per_device,
        mesh=mesh,
        in_specs=(
            P("wide", "narrow", None, None),
            P("wide", "narrow", None),
            P(),
            P(),
            P(),
            P(),
            P(),
            P(),
            P(),
            P(),
            P(),
            P(),
        ),
        out_specs=P("wide", "narrow", None, None),
        check_vma=False,
    )
```

profile of v0, /device:TPU:0, one launch (start us, length us, event | category | flops | bytes accessed | tf_op | source)
XLA Modules:
  0.0 399.7 jit_solution(2876258442550393296)
XLA Ops:
  9.5 4.9 %collective-permute-start = (bf16[1,16,16,512]{3,2,1,0:T(8,128)(2,1)S(1)}, bf16[1,16,16,512]{3,2,1,0:T(8,128)(2,1)S(1)}, u32[]{:S(2)}, u32[]{:S(2)}) collective-permute-start(bf16[1,16,16,512]{3,2,1,0:T(8,128)(2,1)S(1)} %get-tuple-element.11), channel_id=1, source_target_pairs={{0,4},{4,8},{8,12},{12,16},{16,20},{20,24},{24,28},{1,5},{5,9},{9,... | collective-permute-start | bytes 786440 | tf_op jit(solution)/shard_map/ppermute | solution.py:18
  16.6 9.0 %collective-permute-done = bf16[1,16,16,512]{3,2,1,0:T(8,128)(2,1)S(1)} collective-permute-done((bf16[1,16,16,512]{3,2,1,0:T(8,128)(2,1)S(1)}, bf16[1,16,16,512]{3,2,1,0:T(8,128)(2,1)S(1)}, u32[]{:S(2)}, u32[]{:S(2)}) %collective-permute-start) | collective-permute-done | bytes 262176 | tf_op jit(solution)/shard_map/ppermute | solution.py:18
  35.7 16.4 %add_convert_fusion = bf16[8,16,16,512]{3,2,1,0:T(8,128)(2,1)S(1)} fusion(bf16[8,16,16,512]{3,2,1,0:T(8,128)(2,1)S(1)} %broadcast_multiply_fusion, bf16[10,18,18,512]{3,2,1,0:T(8,128)(2,1)S(1)} %select_maximum_fusion, bf16[10,17,16,512]{3,2,1,0:T(8,128)(2,1)S(1)} %get-tuple-element.8, bf16[1,16,16,512]{3,2,1,0:T(8,128)(2,1)S(1)} %collective-permute-done.1, ...), kind=kLoop, calls=%fused_computation.91 | loop fusion | flops 88080384 | bytes 55105536 | tf_op jit(solution)/shard_map/convert_element_type | solution.py:94
  58.8 4.5 %multiply_reduce_fusion.12 = (f32[1024]{0:T(1024)S(1)}, f32[1024,2048]{1,0:T(8,128)}) fusion(bf16[2048,512]{0,1:T(8,128)(2,1)S(1)} %convolution_convert_fusion.1, bf16[1024,512]{0,1:T(8,128)(2,1)S(1)} %convolution_convert_fusion.5), kind=kOutput, calls=%fused_computation.31 | convolution fusion | flops 272628736 | bytes 8785920 | tf_op jit(solution)/shard_map/dot_general | solution.py:33
  63.3 4.5 %multiply_reduce_fusion.13 = (f32[1024]{0:T(1024)S(1)}, f32[1024,2048]{1,0:T(8,128)}) fusion(bf16[2048,512]{0,1:T(8,128)(2,1)S(1)} %convolution_convert_fusion.1, bf16[1024,512]{0,1:T(8,128)(2,1)S(1)} %convolution_convert_fusion.5), kind=kOutput, calls=%fused_computation.32 | convolution fusion | flops 272628736 | bytes 8785920 | tf_op jit(solution)/shard_map/dot_general | solution.py:33
  83.9 7.9 %fusion.149 = f32[1024,512]{0,1:T(8,128)S(1)} fusion(f32[1024,2048]{1,0:T(8,128)} %get-tuple-element.41, f32[1024]{0:T(1024)S(1)} %get-tuple-element.40, bf16[2048,512]{0,1:T(8,128)(2,1)} %convolution_convert_fusion), kind=kOutput, calls=%fused_computation.142 | convolution fusion | flops 1614807040 | bytes 8916992 | tf_op jit(solution)/shard_map/dot_general | solution.py:43
  96.2 8.1 %fusion.148 = f32[1024,512]{0,1:T(8,128)S(1)} fusion(f32[1024,512]{0,1:T(8,128)S(1)} %fusion.149, f32[1024,2048]{1,0:T(8,128)} %get-tuple-element.43, f32[1024]{0:T(1024)S(1)} %get-tuple-element.42, bf16[2048,512]{0,1:T(8,128)(2,1)} %convolution_convert_fusion), kind=kOutput, calls=%fused_computation.141 | convolution fusion | flops 1614807040 | bytes 8916992 | tf_op jit(solution)/shard_map/dot_general | solution.py:43
  108.7 8.1 %fusion.147 = f32[1024,512]{0,1:T(8,128)S(1)} fusion(f32[1024,512]{0,1:T(8,128)S(1)} %fusion.148, f32[1024,2048]{1,0:T(8,128)} %get-tuple-element.45, f32[1024]{0:T(1024)S(1)} %get-tuple-element.44, bf16[2048,512]{0,1:T(8,128)(2,1)} %convolution_convert_fusion), kind=kOutput, calls=%fused_computation.140 | convolution fusion | flops 1614807040 | bytes 8916992 | tf_op jit(solution)/shard_map/dot_general | solution.py:43
  121.1 8.3 %fusion.146 = f32[1024,512]{0,1:T(8,128)S(1)} fusion(f32[1024,512]{0,1:T(8,128)S(1)} %fusion.147, f32[1024,2048]{1,0:T(8,128)} %get-tuple-element.47, f32[1024]{0:T(1024)S(1)} %get-tuple-element.46, bf16[2048,512]{0,1:T(8,128)(2,1)} %convolution_convert_fusion), kind=kOutput, calls=%fused_computation.139 | convolution fusion | flops 1614807040 | bytes 8916992 | tf_op jit(solution)/shard_map/dot_general | solution.py:43
  131.4 6.5 %fusion.145 = f32[1024,512]{0,1:T(8,128)S(1)} fusion(f32[1024,512]{0,1:T(8,128)S(1)} %fusion.146, f32[1024,2048]{1,0:T(8,128)S(1)} %get-tuple-element.49, f32[1024]{0:T(1024)S(1)} %get-tuple-element.48, bf16[2048,512]{0,1:T(8,128)(2,1)} %convolution_convert_fusion), kind=kOutput, calls=%fused_computation.138 | convolution fusion | flops 1614807040 | bytes 8916992 | tf_op jit(solution)/shard_map/dot_general | solution.py:43
  140.2 6.5 %fusion.144 = f32[1024,512]{0,1:T(8,128)S(1)} fusion(f32[1024,512]{0,1:T(8,128)S(1)} %fusion.145, f32[1024,2048]{1,0:T(8,128)S(1)} %get-tuple-element.51, f32[1024]{0:T(1024)S(1)} %get-tuple-element.50, bf16[2048,512]{0,1:T(8,128)(2,1)} %convolution_convert_fusion), kind=kOutput, calls=%fused_computation.137 | convolution fusion | flops 1614807040 | bytes 8916992 | tf_op jit(solution)/shard_map/dot_general | solution.py:43
  154.3 9.5 %all-to-all-start.1 = ((f32[32,1,256]{2,1,0:T(1,128)}), f32[32,1,256]{2,1,0:T(1,128)S(1)}, u32[]{:S(2)}, u32[]{:S(2)}) async-start(f32[32,1,256]{2,1,0:T(1,128)} %reshape.112), calls=%async_computation.1 | async-start | bytes 65536 | tf_op jit(solution)/shard_map/all_to_all | solution.py:121
  163.8 8.1 %fusion.143 = f32[1024,512]{0,1:T(8,128)S(1)} fusion(f32[1024,512]{0,1:T(8,128)S(1)} %fusion.144, f32[1024,2048]{1,0:T(8,128)} %copy-done.3, f32[1024]{0:T(1024)S(1)} %get-tuple-element.52, bf16[2048,512]{0,1:T(8,128)(2,1)} %convolution_convert_fusion), kind=kOutput, calls=%fused_computation.136 | convolution fusion | flops 1614807040 | bytes 8916992 | tf_op jit(solution)/shard_map/dot_general | solution.py:43
  175.1 5.9 %all-to-all-start.2 = ((f32[32,1,256]{2,1,0:T(1,128)}), f32[32,1,256]{2,1,0:T(1,128)S(1)}, u32[]{:S(2)}, u32[]{:S(2)}) async-start(f32[32,1,256]{2,1,0:T(1,128)} %reshape.114), calls=%async_computation.2 | async-start | bytes 65536 | tf_op jit(solution)/shard_map/all_to_all | solution.py:120
  181.1 8.1 %fusion.142 = f32[1024,512]{0,1:T(8,128)S(1)} fusion(f32[1024,512]{0,1:T(8,128)S(1)} %fusion.143, f32[1024,2048]{1,0:T(8,128)} %copy-done.2, f32[1024]{0:T(1024)S(1)} %get-tuple-element.54, bf16[2048,512]{0,1:T(8,128)(2,1)} %convolution_convert_fusion), kind=kOutput, calls=%fused_computation.135 | convolution fusion | flops 1614807040 | bytes 8916992 | tf_op jit(solution)/shard_map/dot_general | solution.py:43
  192.9 6.0 %all-to-all-start = ((f32[1,1024,512]{2,0,1:T(1,128)}), f32[1,1024,512]{2,0,1:T(1,128)}, u32[]{:S(2)}, u32[]{:S(2)}) async-start(f32[1,1024,512]{2,0,1:T(1,128)} %copy.23), calls=%async_computation | async-start | bytes 4194304 | tf_op jit(solution)/shard_map/all_to_all | solution.py:119
  209.5 38.1 %all-to-all-done = f32[1,1024,512]{2,0,1:T(1,128)} async-done(((f32[1,1024,512]{2,0,1:T(1,128)}), f32[1,1024,512]{2,0,1:T(1,128)}, u32[]{:S(2)}, u32[]{:S(2)}) %all-to-all-start) | async-done | bytes 2097184 | tf_op jit(solution)/shard_map/all_to_all | solution.py:119
  254.4 50.3 %all-gather.2.cloned.1.call-done = bf16[1024,512]{1,0:T(8,128)(2,1)} async-done(((bf16[32,512]{1,0:T(8,128)(2,1)}), bf16[1024,512]{1,0:T(8,128)(2,1)}) %all-gather.2.cloned.1.call-update) | async-done | bytes 1048592 | tf_op jit(solution)/shard_map/all_gather | solution.py:136
  310.6 4.5 %multiply_reduce_fusion.3 = (f32[2048]{0:T(1024)S(1)}, f32[2048,1024]{0,1:T(8,128)}) fusion(bf16[1024,512]{0,1:T(8,128)(2,1)S(1)} %convolution_convert_fusion.4, bf16[2048,512]{0,1:T(8,128)(2,1)S(1)} %convolution_convert_fusion.2), kind=kOutput, calls=%fused_computation.22 | convolution fusion | flops 272627712 | bytes 8790016 | tf_op jit(solution)/shard_map/dot_general | solution.py:33
  315.1 4.5 %multiply_reduce_fusion.4 = (f32[2048]{0:T(1024)S(1)}, f32[2048,1024]{0,1:T(8,128)}) fusion(bf16[1024,512]{0,1:T(8,128)(2,1)S(1)} %convolution_convert_fusion.4, bf16[2048,512]{0,1:T(8,128)(2,1)S(1)} %convolution_convert_fusion.2), kind=kOutput, calls=%fused_computation.23 | convolution fusion | flops 272627712 | bytes 8790016 | tf_op jit(solution)/shard_map/dot_general | solution.py:33
  319.6 4.5 %multiply_reduce_fusion.5 = (f32[2048]{0:T(1024)S(1)}, f32[2048,1024]{0,1:T(8,128)}) fusion(bf16[1024,512]{0,1:T(8,128)(2,1)S(1)} %convolution_convert_fusion.4, bf16[2048,512]{0,1:T(8,128)(2,1)S(1)} %convolution_convert_fusion.2), kind=kOutput, calls=%fused_computation.24 | convolution fusion | flops 272627712 | bytes 8790016 | tf_op jit(solution)/shard_map/dot_general | solution.py:33
  324.2 4.5 %multiply_reduce_fusion.6 = (f32[2048]{0:T(1024)S(1)}, f32[2048,1024]{0,1:T(8,128)}) fusion(bf16[1024,512]{0,1:T(8,128)(2,1)S(1)} %convolution_convert_fusion.4, bf16[2048,512]{0,1:T(8,128)(2,1)S(1)} %convolution_convert_fusion.2), kind=kOutput, calls=%fused_computation.25 | convolution fusion | flops 272627712 | bytes 8790016 | tf_op jit(solution)/shard_map/dot_general | solution.py:33
  328.7 5.0 %multiply_reduce_fusion.7 = (f32[2048]{0:T(1024)S(1)}, f32[2048,1024]{0,1:T(8,128)}) fusion(bf16[1024,512]{0,1:T(8,128)(2,1)S(1)} %convolution_convert_fusion.4, bf16[2048,512]{0,1:T(8,128)(2,1)S(1)} %convolution_convert_fusion.2), kind=kOutput, calls=%fused_computation.26 | convolution fusion | flops 272627712 | bytes 8790016 | tf_op jit(solution)/shard_map/dot_general | solution.py:33
  337.9 4.8 %fusion.25 = f32[2048]{0:T(1024)S(1)} fusion(f32[2048,1024]{0,1:T(8,128)} %get-tuple-element.65, f32[2048]{0:T(1024)S(1)} %get-tuple-element.64), kind=kLoop, calls=%fused_computation.59 | loop fusion | flops 6289408 | bytes 8404992 | tf_op jit(solution)/shard_map/reduce_sum | solution.py:149
  342.7 4.8 %fusion.23 = f32[2048]{0:T(1024)S(1)} fusion(f32[2048,1024]{0,1:T(8,128)} %get-tuple-element.63, f32[2048]{0:T(1024)S(1)} %get-tuple-element.62), kind=kLoop, calls=%fused_computation.57 | loop fusion | flops 6289408 | bytes 8404992 | tf_op jit(solution)/shard_map/reduce_sum | solution.py:149
  347.4 4.8 %fusion.21 = f32[2048]{0:T(1024)S(1)} fusion(f32[2048,1024]{0,1:T(8,128)} %get-tuple-element.61, f32[2048]{0:T(1024)S(1)} %get-tuple-element.60), kind=kLoop, calls=%fused_computation.55 | loop fusion | flops 6289408 | bytes 8404992 | tf_op jit(solution)/shard_map/reduce_sum | solution.py:149
  352.2 4.8 %fusion.19 = f32[2048]{0:T(1024)S(1)} fusion(f32[2048,1024]{0,1:T(8,128)} %get-tuple-element.59, f32[2048]{0:T(1024)S(1)} %get-tuple-element.58), kind=kLoop, calls=%fused_computation.53 | loop fusion | flops 6289408 | bytes 8404992 | tf_op jit(solution)/shard_map/reduce_sum | solution.py:149
  357.0 5.1 %fusion.17 = f32[2048]{0:T(1024)S(1)} fusion(f32[2048,1024]{0,1:T(8,128)} %get-tuple-element.57, f32[2048]{0:T(1024)S(1)} %get-tuple-element.56), kind=kLoop, calls=%fused_computation.51 | loop fusion | flops 6289408 | bytes 8404992 | tf_op jit(solution)/shard_map/reduce_sum | solution.py:149
  362.9 4.9 %fusion.76 = bf16[2048,512]{0,1:T(8,128)(2,1)S(1)} fusion(f32[2048,1024]{0,1:T(8,128)} %get-tuple-element.57, f32[2048]{0:T(1024)S(1)} %get-tuple-element.56, f32[2048]{0:T(1024)S(1)} %fusion.17, bf16[1024,512]{0,1:T(8,128)(2,1)S(1)} %convolution_convert_fusion.3), kind=kOutput, calls=%fused_computation.107 | convolution fusion | flops 274989056 | bytes 8798208 | tf_op jit(solution)/shard_map/dot_general | solution.py:150
  367.8 4.9 %fusion.85 = bf16[2048,512]{0,1:T(8,128)(2,1)S(1)} fusion(bf16[2048,512]{0,1:T(8,128)(2,1)S(1)} %fusion.76, f32[2048,1024]{0,1:T(8,128)} %get-tuple-element.59, f32[2048]{0:T(1024)S(1)} %get-tuple-element.58, f32[2048]{0:T(1024)S(1)} %fusion.19, bf16[1024,512]{0,1:T(8,128)(2,1)S(1)} %convolution_convert_fusion.3), kind=kOutput, calls=%fused_computation.110 | convolution fusion | flops 274989056 | bytes 8798208 | tf_op jit(solution)/shard_map/dot_general | solution.py:150
  372.8 5.1 %fusion.94 = bf16[2048,512]{0,1:T(8,128)(2,1)S(1)} fusion(bf16[2048,512]{0,1:T(8,128)(2,1)S(1)} %fusion.85, f32[2048,1024]{0,1:T(8,128)} %get-tuple-element.61, f32[2048]{0:T(1024)S(1)} %get-tuple-element.60, f32[2048]{0:T(1024)S(1)} %fusion.21, bf16[1024,512]{0,1:T(8,128)(2,1)S(1)} %convolution_convert_fusion.3), kind=kOutput, calls=%fused_computation.113 | convolution fusion | flops 274989056 | bytes 8798208 | tf_op jit(solution)/shard_map/dot_general | solution.py:150
  377.8 5.1 %fusion.103 = bf16[2048,512]{0,1:T(8,128)(2,1)S(1)} fusion(bf16[2048,512]{0,1:T(8,128)(2,1)S(1)} %fusion.94, f32[2048,1024]{0,1:T(8,128)} %get-tuple-element.63, f32[2048]{0:T(1024)S(1)} %get-tuple-element.62, f32[2048]{0:T(1024)S(1)} %fusion.23, bf16[1024,512]{0,1:T(8,128)(2,1)S(1)} %convolution_convert_fusion.3), kind=kOutput, calls=%fused_computation.116 | convolution fusion | flops 274989056 | bytes 8798208 | tf_op jit(solution)/shard_map/dot_general | solution.py:150
  (116 shorter events, 107.6 us)
Async XLA Ops:
  6.5 45.5 %copy-start = (bf16[512,512]{1,0:T(8,128)(2,1)S(1)}, bf16[512,512]{1,0:T(8,128)(2,1)}, u32[]{:S(2)}) copy-start(bf16[512,512]{1,0:T(8,128)(2,1)} %param.17) | copy-start | bytes 1572868
  6.5 9.2 %copy-start.9 = (f32[27,512]{1,0:T(8,128)S(1)}, f32[27,512]{1,0:T(8,128)}, u32[]{:S(2)}) copy-start(f32[27,512]{1,0:T(8,128)} %param.14) | copy-start | bytes 165892
  6.5 9.2 %copy-start.10 = (bf16[1024,512]{1,0:T(8,128)(2,1)S(1)}, bf16[1024,512]{1,0:T(8,128)(2,1)}, u32[]{:S(2)}) copy-start(bf16[1024,512]{1,0:T(8,128)(2,1)} %param.15) | copy-start | bytes 3145732
  6.5 9.2 %copy-start.12 = (bf16[512,512]{1,0:T(8,128)(2,1)S(1)}, bf16[512,512]{1,0:T(8,128)(2,1)}, u32[]{:S(2)}) copy-start(bf16[512,512]{1,0:T(8,128)(2,1)} %param.16) | copy-start | bytes 1572868
  9.5 26.2 %copy-start.4 = (bf16[8,16,16,512]{3,2,1,0:T(8,128)(2,1)}, bf16[8,16,16,512]{3,2,1,0:T(8,128)(2,1)S(1)}, u32[]{:S(2)}) copy-start(bf16[8,16,16,512]{3,2,1,0:T(8,128)(2,1)S(1)} %broadcast_multiply_fusion) | copy-start | bytes 6291460
  9.5 16.0 %collective-permute-start = (bf16[1,16,16,512]{3,2,1,0:T(8,128)(2,1)S(1)}, bf16[1,16,16,512]{3,2,1,0:T(8,128)(2,1)S(1)}, u32[]{:S(2)}, u32[]{:S(2)}) collective-permute-start(bf16[1,16,16,512]{3,2,1,0:T(8,128)(2,1)S(1)} %get-tuple-element.11), channel_id=1, source_target_pairs={{0,4},{4,8},{8,12},{12,16},{16,20},{20,24},{24,28},{1,5},{5,9},{9,... | collective-permute-start | bytes 786440 | tf_op jit(solution)/shard_map/ppermute | solution.py:18
  14.4 11.2 %collective-permute-start.1 = (bf16[1,16,16,512]{3,2,1,0:T(8,128)(2,1)S(1)}, bf16[1,16,16,512]{3,2,1,0:T(8,128)(2,1)S(1)}, u32[]{:S(2)}, u32[]{:S(2)}) collective-permute-start(bf16[1,16,16,512]{3,2,1,0:T(8,128)(2,1)S(1)} %get-tuple-element.12), channel_id=1, source_target_pairs={{4,0},{8,4},{12,8},{16,12},{20,16},{24,20},{28,24},{5,1},{9,5},{13... | collective-permute-start | bytes 786440 | tf_op jit(solution)/shard_map/ppermute | solution.py:20
  25.6 2.6 collective-permute-start.2
  26.9 5.0 %collective-permute-start.3 = (bf16[10,1,16,512]{3,2,1,0:T(8,128)(2,1)S(1)}, bf16[10,1,16,512]{3,2,1,0:T(8,128)(2,1)S(1)}, u32[]{:S(2)}, u32[]{:S(2)}) collective-permute-start(bf16[10,1,16,512]{3,2,1,0:T(8,128)(2,1)S(1)} %get-tuple-element.10), channel_id=1, source_target_pairs={{1,0},{2,1},{3,2},{5,4},{6,5},{7,6},{9,8},{10,9},{11,10},{13,12},{... | collective-permute-start | bytes 491528 | tf_op jit(solution)/shard_map/ppermute | solution.py:20
  52.1 24.7 %copy-start.6 = (bf16[8,16,16,512]{3,2,1,0:T(8,128)(2,1)}, bf16[8,16,16,512]{3,2,1,0:T(8,128)(2,1)S(1)}, u32[]{:S(2)}) copy-start(bf16[8,16,16,512]{3,2,1,0:T(8,128)(2,1)S(1)} %add_convert_fusion) | copy-start | bytes 6291460
  54.7 92.0 %copy-start.2 = (f32[1024,2048]{1,0:T(8,128)}, f32[1024,2048]{1,0:T(8,128)S(1)}, u32[]{:S(2)}) copy-start(f32[1024,2048]{1,0:T(8,128)S(1)} %get-tuple-element.55) | copy-start | bytes 25165828
  56.1 92.5 %copy-start.3 = (f32[1024,2048]{1,0:T(8,128)}, f32[1024,2048]{1,0:T(8,128)S(1)}, u32[]{:S(2)}) copy-start(f32[1024,2048]{1,0:T(8,128)S(1)} %get-tuple-element.53) | copy-start | bytes 25165828
  72.3 4.5 %copy-start.13 = (bf16[512,512]{1,0:T(8,128)(2,1)S(1)}, bf16[512,512]{1,0:T(8,128)(2,1)}, u32[]{:S(2)}) copy-start(bf16[512,512]{1,0:T(8,128)(2,1)} %param.18) | copy-start | bytes 1572868
  154.3 20.8 %all-to-all-start.1 = ((f32[32,1,256]{2,1,0:T(1,128)}), f32[32,1,256]{2,1,0:T(1,128)S(1)}, u32[]{:S(2)}, u32[]{:S(2)}) async-start(f32[32,1,256]{2,1,0:T(1,128)} %reshape.112), calls=%async_computation.1 | async-start | bytes 65536 | tf_op jit(solution)/shard_map/all_to_all | solution.py:121
  175.1 17.8 %all-to-all-start.2 = ((f32[32,1,256]{2,1,0:T(1,128)}), f32[32,1,256]{2,1,0:T(1,128)S(1)}, u32[]{:S(2)}, u32[]{:S(2)}) async-start(f32[32,1,256]{2,1,0:T(1,128)} %reshape.114), calls=%async_computation.2 | async-start | bytes 65536 | tf_op jit(solution)/shard_map/all_to_all | solution.py:120
  192.9 54.7 %all-to-all-start = ((f32[1,1024,512]{2,0,1:T(1,128)}), f32[1,1024,512]{2,0,1:T(1,128)}, u32[]{:S(2)}, u32[]{:S(2)}) async-start(f32[1,1024,512]{2,0,1:T(1,128)} %copy.23), calls=%async_computation | async-start | bytes 4194304 | tf_op jit(solution)/shard_map/all_to_all | solution.py:119
  198.9 105.8 %all-gather.2.cloned.1.call-start = ((), (), s32[]{:S(2)}) async-start(), calls=%async_computation.3 | async-start | bytes 1081344 | tf_op jit(solution)/shard_map/all_gather | solution.py:136
  209.4 40.4 %copy-start.8 = (bf16[512,512]{1,0:T(8,128)(2,1)S(1)}, bf16[512,512]{1,0:T(8,128)(2,1)}, u32[]{:S(2)}) copy-start(bf16[512,512]{1,0:T(8,128)(2,1)} %param.19) | copy-start | bytes 1572868
  209.5 42.0 %copy-start.14 = (bf16[512,512]{1,0:T(8,128)(2,1)S(1)}, bf16[512,512]{1,0:T(8,128)(2,1)}, u32[]{:S(2)}) copy-start(bf16[512,512]{1,0:T(8,128)(2,1)} %param.20) | copy-start | bytes 1572868
  251.4 53.2 %copy-start.15 = (bf16[512,512]{1,0:T(8,128)(2,1)S(1)}, bf16[512,512]{1,0:T(8,128)(2,1)}, u32[]{:S(2)}) copy-start(bf16[512,512]{1,0:T(8,128)(2,1)} %param.21) | copy-start | bytes 1572868
  357.0 5.1 %copy-start.11 = (bf16[1024,512]{1,0:T(8,128)(2,1)S(1)}, bf16[1024,512]{1,0:T(8,128)(2,1)}, u32[]{:S(2)}) copy-start(bf16[1024,512]{1,0:T(8,128)(2,1)} %all-gather.2.cloned.1.call-done) | copy-start | bytes 3145732
  357.0 5.1 %copy-start.16 = (bf16[512,512]{1,0:T(8,128)(2,1)S(1)}, bf16[512,512]{1,0:T(8,128)(2,1)}, u32[]{:S(2)}) copy-start(bf16[512,512]{1,0:T(8,128)(2,1)} %param.22) | copy-start | bytes 1572868
  372.7 10.2 %slice-start = ((s8[8388608]{0:T(1024)(128)(4,1)}), s8[4194304]{0:T(1024)(128)(4,1)S(1)}, s32[]{:S(2)}) async-start(s8[8388608]{0:T(1024)(128)(4,1)} %bitcast.74), calls=%async_computation.4 | async-start | bytes 8388608
  377.8 5.1 %slice-start.1 = ((s8[8388608]{0:T(1024)(128)(4,1)}), s8[4194304]{0:T(1024)(128)(4,1)S(1)}, s32[]{:S(2)}) async-start(s8[8388608]{0:T(1024)(128)(4,1)} %bitcast.74), calls=%async_computation.5 | async-start | bytes 8388608
  387.6 1.6 copy-start.5
  387.6 1.7 copy-start.7
  387.6 5.0 %copy-start.1 = (bf16[512,512]{1,0:T(8,128)(2,1)S(1)}, bf16[512,512]{1,0:T(8,128)(2,1)}, u32[]{:S(2)}) copy-start(bf16[512,512]{1,0:T(8,128)(2,1)} %param.17) | copy-start | bytes 1572868
Sparse Core Ops, SparseCore 0:
  251.5 53.0 all-gather.1
where the time goes:
time: 405 us; the launch traced here: 400 us
  matrix products  154 us (38%)
  waiting for transfers between devices  101 us (25%)
  other arithmetic  82.8 us (20%)
  starting transfers between devices  30.2 us (7%)
  local copies, waits for them, and re-layouts  17.8 us (4%)
  between operations  14.2 us (4%)
    dot_general x8, matrix products, exact_dot(): jnp.dot(weights, values_block, precision=lax.Precision.HIGHEST, preferred...  61.6 us
    dot_general x16, matrix products, pair_scores(): lax.dot_general(queries, key_rows, (((1,), (1,)), ((), ())), preferred_el...  50.3 us
    all_gather x1, waiting for transfers between devices, per_device(): lax.all_gather(own_state, ('wide', 'narrow'), axis=0, tiled=True)  50.3 us
    all_to_all x1, waiting for transfers between devices, per_device(): lax.all_to_all(summed1, ('wide', 'narrow'), split_axis=1, concat_axis=0,...  38.1 us
    reduce_sum x8, other arithmetic, per_device(): totals = jnp.sum(weights, axis=1, keepdims=True)  28.4 us
    dot_general x8, matrix products, per_device(): jnp.dot(weights.astype(jnp.bfloat16), head_block(values2, head_index, hea...  26.2 us
    reduce_sum x8, other arithmetic, per_device(): totals_list.append(jnp.sum(weights, axis=1))  25.6 us
    convert_element_type x1, other arithmetic, per_device(): mixed_cells = stencil.astype(jnp.bfloat16).reshape(cell_count, model_width)  16.4 us
  transfers between devices with their start and end apart: 8, of which 4 were waited for; matrix products, arithmetic and copies ran while one was open for 9% of the time, Pallas kernels for 0%

commit v1 on v0

--- a/solution.py
+++ b/solution.py
@@ -133,7 +133,16 @@
     ) * row_count
     own_latents = lax.dynamic_slice_in_dim(latents, start, row_count, 0)
     own_state = update_state(summed, totals, own_latents, w_out1, head_count)
-    latent_state = lax.all_gather(own_state, ("wide", "narrow"), axis=0, tiled=True)
+    ways, here = (lax.axis_size(("wide", "narrow")), lax.axis_index(("wide", "narrow")))
+    latent_state, reach = (own_state, 1)
+    while reach < ways:
+        theirs = lax.ppermute(
+            latent_state, ("wide", "narrow"), [(d, d ^ reach) for d in range(ways)]
+        )
+        mine_first = jnp.concatenate([latent_state, theirs], axis=0)
+        theirs_first = jnp.concatenate([theirs, latent_state], axis=0)
+        latent_state = jnp.where(here & reach == 0, mine_first, theirs_first)
+        reach = 2 * reach
     keys2 = project(latent_state, w_key2)
     values2 = project(latent_state, w_value2)
     queries2 = project(mixed_cells, w_query2)

time: 405 us -> 376 us (0.928)
  waiting for transfers between devices: 101 us -> 83.2 us
  between operations: 14.2 us -> 0.79 us
  starting transfers between devices: 30.2 us -> 34.6 us
    all_gather x1 -> x0, waiting for transfers between devices: 50.3 us -> none  [per_device(): lax.all_gather(own_state, ('wide', 'narrow'), axis=0, tiled=True)]
    ppermute x0 -> x5, waiting for transfers between devices: none -> 32.4 us  [per_device(): lax.ppermute(latent_state, ('wide', 'narrow'), [(d, d ^ reach) for d in r...]
    ppermute x0 -> x5, starting transfers between devices: none -> 4.43 us  [per_device(): lax.ppermute(latent_state, ('wide', 'narrow'), [(d, d ^ reach) for d in r...]
  transfers between devices with their start and end apart: 8 -> 12, of which waited for: 4 -> 8; matrix products, arithmetic and copies ran while one was open for 9% -> 10% of each run, Pallas kernels for 0% -> 0%
where the time goes in v1:
time: 376 us; the launch traced here: 371 us
  matrix products  152 us (40%)
  waiting for transfers between devices  83.2 us (22%)
  other arithmetic  83.1 us (22%)
  starting transfers between devices  34.6 us (9%)
  local copies, waits for them, and re-layouts  17.8 us (5%)
    dot_general x8, matrix products, exact_dot(): jnp.dot(weights, values_block, precision=lax.Precision.HIGHEST, preferred...  61.6 us
    dot_general x16, matrix products, pair_scores(): lax.dot_general(queries, key_rows, (((1,), (1,)), ((), ())), preferred_el...  50.3 us
    all_to_all x1, waiting for transfers between devices, per_device(): lax.all_to_all(summed1, ('wide', 'narrow'), split_axis=1, concat_axis=0,...  38.1 us
    ppermute x5, waiting for transfers between devices, per_device(): lax.ppermute(latent_state, ('wide', 'narrow'), [(d, d ^ reach) for d in r...  32.4 us
    reduce_sum x8, other arithmetic, per_device(): totals = jnp.sum(weights, axis=1, keepdims=True)  28.4 us
    dot_general x8, matrix products, per_device(): jnp.dot(weights.astype(jnp.bfloat16), head_block(values2, head_index, hea...  26.2 us
    reduce_sum x8, other arithmetic, per_device(): totals_list.append(jnp.sum(weights, axis=1))  25.6 us
    convert_element_type x1, other arithmetic, per_device(): mixed_cells = stencil.astype(jnp.bfloat16).reshape(cell_count, model_width)  16.4 us
  transfers between devices with their start and end apart: 12, of which 8 were waited for; matrix products, arithmetic and copies ran while one was open for 10% of the time, Pallas kernels for 0%

profile of v1, /device:TPU:0, one launch (start us, length us, event | category | flops | bytes accessed | tf_op | source)
XLA Modules:
  0.0 371.2 jit_solution(16370202451617796810)
XLA Ops:
  3.0 4.9 %collective-permute-start = (bf16[1,16,16,512]{3,2,1,0:T(8,128)(2,1)S(1)}, bf16[1,16,16,512]{3,2,1,0:T(8,128)(2,1)S(1)}, u32[]{:S(2)}, u32[]{:S(2)}) collective-permute-start(bf16[1,16,16,512]{3,2,1,0:T(8,128)(2,1)S(1)} %get-tuple-element.11), channel_id=1, source_target_pairs={{0,4},{4,8},{8,12},{12,16},{16,20},{20,24},{24,28},{1,5},{5,9},{9,... | collective-permute-start | bytes 786440 | tf_op jit(solution)/shard_map/ppermute | solution.py:18
  10.0 9.0 %collective-permute-done = bf16[1,16,16,512]{3,2,1,0:T(8,128)(2,1)S(1)} collective-permute-done((bf16[1,16,16,512]{3,2,1,0:T(8,128)(2,1)S(1)}, bf16[1,16,16,512]{3,2,1,0:T(8,128)(2,1)S(1)}, u32[]{:S(2)}, u32[]{:S(2)}) %collective-permute-start) | collective-permute-done | bytes 262176 | tf_op jit(solution)/shard_map/ppermute | solution.py:18
  29.2 16.4 %add_convert_fusion = bf16[8,16,16,512]{3,2,1,0:T(8,128)(2,1)S(1)} fusion(bf16[8,16,16,512]{3,2,1,0:T(8,128)(2,1)S(1)} %broadcast_multiply_fusion, bf16[10,18,18,512]{3,2,1,0:T(8,128)(2,1)S(1)} %select_maximum_fusion, bf16[10,17,16,512]{3,2,1,0:T(8,128)(2,1)S(1)} %get-tuple-element.8, bf16[1,16,16,512]{3,2,1,0:T(8,128)(2,1)S(1)} %collective-permute-done.1, ...), kind=kLoop, calls=%fused_computation.91 | loop fusion | flops 88080384 | bytes 55105536 | tf_op jit(solution)/shard_map/convert_element_type | solution.py:94
  52.3 4.5 %multiply_reduce_fusion.12 = (f32[1024]{0:T(1024)S(1)}, f32[1024,2048]{1,0:T(8,128)}) fusion(bf16[2048,512]{0,1:T(8,128)(2,1)S(1)} %convolution_convert_fusion.1, bf16[1024,512]{0,1:T(8,128)(2,1)S(1)} %convolution_convert_fusion.5), kind=kOutput, calls=%fused_computation.31 | convolution fusion | flops 272628736 | bytes 8785920 | tf_op jit(solution)/shard_map/dot_general | solution.py:33
  77.4 7.9 %fusion.149 = f32[1024,512]{0,1:T(8,128)S(1)} fusion(f32[1024,2048]{1,0:T(8,128)} %get-tuple-element.41, f32[1024]{0:T(1024)S(1)} %get-tuple-element.40, bf16[2048,512]{0,1:T(8,128)(2,1)} %convolution_convert_fusion), kind=kOutput, calls=%fused_computation.142 | convolution fusion | flops 1614807040 | bytes 8916992 | tf_op jit(solution)/shard_map/dot_general | solution.py:43
  89.7 8.1 %fusion.148 = f32[1024,512]{0,1:T(8,128)S(1)} fusion(f32[1024,512]{0,1:T(8,128)S(1)} %fusion.149, f32[1024,2048]{1,0:T(8,128)} %get-tuple-element.43, f32[1024]{0:T(1024)S(1)} %get-tuple-element.42, bf16[2048,512]{0,1:T(8,128)(2,1)} %convolution_convert_fusion), kind=kOutput, calls=%fused_computation.141 | convolution fusion | flops 1614807040 | bytes 8916992 | tf_op jit(solution)/shard_map/dot_general | solution.py:43
  102.1 8.1 %fusion.147 = f32[1024,512]{0,1:T(8,128)S(1)} fusion(f32[1024,512]{0,1:T(8,128)S(1)} %fusion.148, f32[1024,2048]{1,0:T(8,128)} %get-tuple-element.45, f32[1024]{0:T(1024)S(1)} %get-tuple-element.44, bf16[2048,512]{0,1:T(8,128)(2,1)} %convolution_convert_fusion), kind=kOutput, calls=%fused_computation.140 | convolution fusion | flops 1614807040 | bytes 8916992 | tf_op jit(solution)/shard_map/dot_general | solution.py:43
  114.6 8.3 %fusion.146 = f32[1024,512]{0,1:T(8,128)S(1)} fusion(f32[1024,512]{0,1:T(8,128)S(1)} %fusion.147, f32[1024,2048]{1,0:T(8,128)} %get-tuple-element.47, f32[1024]{0:T(1024)S(1)} %get-tuple-element.46, bf16[2048,512]{0,1:T(8,128)(2,1)} %convolution_convert_fusion), kind=kOutput, calls=%fused_computation.139 | convolution fusion | flops 1614807040 | bytes 8916992 | tf_op jit(solution)/shard_map/dot_general | solution.py:43
  124.9 6.5 %fusion.145 = f32[1024,512]{0,1:T(8,128)S(1)} fusion(f32[1024,512]{0,1:T(8,128)S(1)} %fusion.146, f32[1024,2048]{1,0:T(8,128)S(1)} %get-tuple-element.49, f32[1024]{0:T(1024)S(1)} %get-tuple-element.48, bf16[2048,512]{0,1:T(8,128)(2,1)} %convolution_convert_fusion), kind=kOutput, calls=%fused_computation.138 | convolution fusion | flops 1614807040 | bytes 8916992 | tf_op jit(solution)/shard_map/dot_general | solution.py:43
  133.7 6.5 %fusion.144 = f32[1024,512]{0,1:T(8,128)S(1)} fusion(f32[1024,512]{0,1:T(8,128)S(1)} %fusion.145, f32[1024,2048]{1,0:T(8,128)S(1)} %get-tuple-element.51, f32[1024]{0:T(1024)S(1)} %get-tuple-element.50, bf16[2048,512]{0,1:T(8,128)(2,1)} %convolution_convert_fusion), kind=kOutput, calls=%fused_computation.137 | convolution fusion | flops 1614807040 | bytes 8916992 | tf_op jit(solution)/shard_map/dot_general | solution.py:43
  147.8 9.5 %all-to-all-start.1 = ((f32[32,1,256]{2,1,0:T(1,128)}), f32[32,1,256]{2,1,0:T(1,128)S(1)}, u32[]{:S(2)}, u32[]{:S(2)}) async-start(f32[32,1,256]{2,1,0:T(1,128)} %reshape.112), calls=%async_computation.1 | async-start | bytes 65536 | tf_op jit(solution)/shard_map/all_to_all | solution.py:121
  157.3 8.1 %fusion.143 = f32[1024,512]{0,1:T(8,128)S(1)} fusion(f32[1024,512]{0,1:T(8,128)S(1)} %fusion.144, f32[1024,2048]{1,0:T(8,128)} %copy-done.3, f32[1024]{0:T(1024)S(1)} %get-tuple-element.52, bf16[2048,512]{0,1:T(8,128)(2,1)} %convolution_convert_fusion), kind=kOutput, calls=%fused_computation.136 | convolution fusion | flops 1614807040 | bytes 8916992 | tf_op jit(solution)/shard_map/dot_general | solution.py:43
  168.6 5.9 %all-to-all-start.2 = ((f32[32,1,256]{2,1,0:T(1,128)}), f32[32,1,256]{2,1,0:T(1,128)S(1)}, u32[]{:S(2)}, u32[]{:S(2)}) async-start(f32[32,1,256]{2,1,0:T(1,128)} %reshape.114), calls=%async_computation.2 | async-start | bytes 65536 | tf_op jit(solution)/shard_map/all_to_all | solution.py:120
  174.6 8.1 %fusion.142 = f32[1024,512]{0,1:T(8,128)S(1)} fusion(f32[1024,512]{0,1:T(8,128)S(1)} %fusion.143, f32[1024,2048]{1,0:T(8,128)} %copy-done.2, f32[1024]{0:T(1024)S(1)} %get-tuple-element.54, bf16[2048,512]{0,1:T(8,128)(2,1)} %convolution_convert_fusion), kind=kOutput, calls=%fused_computation.135 | convolution fusion | flops 1614807040 | bytes 8916992 | tf_op jit(solution)/shard_map/dot_general | solution.py:43
  186.4 6.0 %all-to-all-start = ((f32[1,1024,512]{2,0,1:T(1,128)}), f32[1,1024,512]{2,0,1:T(1,128)}, u32[]{:S(2)}, u32[]{:S(2)}) async-start(f32[1,1024,512]{2,0,1:T(1,128)} %copy.23), calls=%async_computation | async-start | bytes 4194304 | tf_op jit(solution)/shard_map/all_to_all | solution.py:119
  202.9 38.1 %all-to-all-done = f32[1,1024,512]{2,0,1:T(1,128)} async-done(((f32[1,1024,512]{2,0,1:T(1,128)}), f32[1,1024,512]{2,0,1:T(1,128)}, u32[]{:S(2)}, u32[]{:S(2)}) %all-to-all-start) | async-done | bytes 2097184 | tf_op jit(solution)/shard_map/all_to_all | solution.py:119
  255.2 6.2 %collective-permute-done.7 = bf16[256,512]{1,0:T(8,128)(2,1)S(1)} collective-permute-done((bf16[256,512]{1,0:T(8,128)(2,1)S(1)}, bf16[256,512]{1,0:T(8,128)(2,1)S(1)}, u32[]{:S(2)}, u32[]{:S(2)}) %collective-permute-start.7) | collective-permute-done | bytes 262176 | tf_op jit(solution)/shard_map/ppermute | solution.py:139
  265.8 18.6 %collective-permute-done.8 = bf16[512,512]{1,0:T(8,128)(2,1)S(1)} collective-permute-done((bf16[512,512]{1,0:T(8,128)(2,1)S(1)}, bf16[512,512]{1,0:T(8,128)(2,1)S(1)}, u32[]{:S(2)}, u32[]{:S(2)}) %collective-permute-start.8) | collective-permute-done | bytes 524320 | tf_op jit(solution)/shard_map/ppermute | solution.py:139
  289.1 4.5 %multiply_reduce_fusion.3 = (f32[2048]{0:T(1024)S(1)}, f32[2048,1024]{0,1:T(8,128)}) fusion(bf16[1024,512]{0,1:T(8,128)(2,1)S(1)} %convolution_convert_fusion.4, bf16[2048,512]{0,1:T(8,128)(2,1)S(1)} %convolution_convert_fusion.2), kind=kOutput, calls=%fused_computation.22 | convolution fusion | flops 272627712 | bytes 8790016 | tf_op jit(solution)/shard_map/dot_general | solution.py:33
  293.6 4.5 %multiply_reduce_fusion.4 = (f32[2048]{0:T(1024)S(1)}, f32[2048,1024]{0,1:T(8,128)}) fusion(bf16[1024,512]{0,1:T(8,128)(2,1)S(1)} %convolution_convert_fusion.4, bf16[2048,512]{0,1:T(8,128)(2,1)S(1)} %convolution_convert_fusion.2), kind=kOutput, calls=%fused_computation.23 | convolution fusion | flops 272627712 | bytes 8790016 | tf_op jit(solution)/shard_map/dot_general | solution.py:33
  298.1 4.5 %multiply_reduce_fusion.5 = (f32[2048]{0:T(1024)S(1)}, f32[2048,1024]{0,1:T(8,128)}) fusion(bf16[1024,512]{0,1:T(8,128)(2,1)S(1)} %convolution_convert_fusion.4, bf16[2048,512]{0,1:T(8,128)(2,1)S(1)} %convolution_convert_fusion.2), kind=kOutput, calls=%fused_computation.24 | convolution fusion | flops 272627712 | bytes 8790016 | tf_op jit(solution)/shard_map/dot_general | solution.py:33
  302.6 5.0 %multiply_reduce_fusion.6 = (f32[2048]{0:T(1024)S(1)}, f32[2048,1024]{0,1:T(8,128)}) fusion(bf16[1024,512]{0,1:T(8,128)(2,1)S(1)} %convolution_convert_fusion.4, bf16[2048,512]{0,1:T(8,128)(2,1)S(1)} %convolution_convert_fusion.2), kind=kOutput, calls=%fused_computation.25 | convolution fusion | flops 272627712 | bytes 8790016 | tf_op jit(solution)/shard_map/dot_general | solution.py:33
  307.6 4.5 %multiply_reduce_fusion.7 = (f32[2048]{0:T(1024)S(1)}, f32[2048,1024]{0,1:T(8,128)}) fusion(bf16[1024,512]{0,1:T(8,128)(2,1)S(1)} %convolution_convert_fusion.4, bf16[2048,512]{0,1:T(8,128)(2,1)S(1)} %convolution_convert_fusion.2), kind=kOutput, calls=%fused_computation.26 | convolution fusion | flops 272627712 | bytes 8790016 | tf_op jit(solution)/shard_map/dot_general | solution.py:33
  316.3 4.8 %fusion.25 = f32[2048]{0:T(1024)S(1)} fusion(f32[2048,1024]{0,1:T(8,128)} %get-tuple-element.65, f32[2048]{0:T(1024)S(1)} %get-tuple-element.64), kind=kLoop, calls=%fused_computation.59 | loop fusion | flops 6289408 | bytes 8404992 | tf_op jit(solution)/shard_map/reduce_sum | solution.py:158
  321.1 4.8 %fusion.23 = f32[2048]{0:T(1024)S(1)} fusion(f32[2048,1024]{0,1:T(8,128)} %get-tuple-element.63, f32[2048]{0:T(1024)S(1)} %get-tuple-element.62), kind=kLoop, calls=%fused_computation.57 | loop fusion | flops 6289408 | bytes 8404992 | tf_op jit(solution)/shard_map/reduce_sum | solution.py:158
  325.9 4.8 %fusion.21 = f32[2048]{0:T(1024)S(1)} fusion(f32[2048,1024]{0,1:T(8,128)} %get-tuple-element.61, f32[2048]{0:T(1024)S(1)} %get-tuple-element.60), kind=kLoop, calls=%fused_computation.55 | loop fusion | flops 6289408 | bytes 8404992 | tf_op jit(solution)/shard_map/reduce_sum | solution.py:158
  330.7 4.8 %fusion.19 = f32[2048]{0:T(1024)S(1)} fusion(f32[2048,1024]{0,1:T(8,128)} %get-tuple-element.59, f32[2048]{0:T(1024)S(1)} %get-tuple-element.58), kind=kLoop, calls=%fused_computation.53 | loop fusion | flops 6289408 | bytes 8404992 | tf_op jit(solution)/shard_map/reduce_sum | solution.py:158
  335.5 5.0 %fusion.17 = f32[2048]{0:T(1024)S(1)} fusion(f32[2048,1024]{0,1:T(8,128)} %get-tuple-element.57, f32[2048]{0:T(1024)S(1)} %get-tuple-element.56), kind=kLoop, calls=%fused_computation.51 | loop fusion | flops 6289408 | bytes 8404992 | tf_op jit(solution)/shard_map/reduce_sum | solution.py:158
  341.3 4.9 %fusion.76 = bf16[2048,512]{0,1:T(8,128)(2,1)S(1)} fusion(f32[2048,1024]{0,1:T(8,128)} %get-tuple-element.57, f32[2048]{0:T(1024)S(1)} %get-tuple-element.56, f32[2048]{0:T(1024)S(1)} %fusion.17, bf16[1024,512]{0,1:T(8,128)(2,1)S(1)} %convolution_convert_fusion.3), kind=kOutput, calls=%fused_computation.107 | convolution fusion | flops 274989056 | bytes 8798208 | tf_op jit(solution)/shard_map/dot_general | solution.py:159
  346.2 4.9 %fusion.85 = bf16[2048,512]{0,1:T(8,128)(2,1)S(1)} fusion(bf16[2048,512]{0,1:T(8,128)(2,1)S(1)} %fusion.76, f32[2048,1024]{0,1:T(8,128)} %get-tuple-element.59, f32[2048]{0:T(1024)S(1)} %get-tuple-element.58, f32[2048]{0:T(1024)S(1)} %fusion.19, bf16[1024,512]{0,1:T(8,128)(2,1)S(1)} %convolution_convert_fusion.3), kind=kOutput, calls=%fused_computation.110 | convolution fusion | flops 274989056 | bytes 8798208 | tf_op jit(solution)/shard_map/dot_general | solution.py:159
  351.1 5.1 %fusion.94 = bf16[2048,512]{0,1:T(8,128)(2,1)S(1)} fusion(bf16[2048,512]{0,1:T(8,128)(2,1)S(1)} %fusion.85, f32[2048,1024]{0,1:T(8,128)} %get-tuple-element.61, f32[2048]{0:T(1024)S(1)} %get-tuple-element.60, f32[2048]{0:T(1024)S(1)} %fusion.21, bf16[1024,512]{0,1:T(8,128)(2,1)S(1)} %convolution_convert_fusion.3), kind=kOutput, calls=%fused_computation.113 | convolution fusion | flops 274989056 | bytes 8798208 | tf_op jit(solution)/shard_map/dot_general | solution.py:159
  356.2 5.1 %fusion.103 = bf16[2048,512]{0,1:T(8,128)(2,1)S(1)} fusion(bf16[2048,512]{0,1:T(8,128)(2,1)S(1)} %fusion.94, f32[2048,1024]{0,1:T(8,128)} %get-tuple-element.63, f32[2048]{0:T(1024)S(1)} %get-tuple-element.62, f32[2048]{0:T(1024)S(1)} %fusion.23, bf16[1024,512]{0,1:T(8,128)(2,1)S(1)} %convolution_convert_fusion.3), kind=kOutput, calls=%fused_computation.116 | convolution fusion | flops 274989056 | bytes 8798208 | tf_op jit(solution)/shard_map/dot_general | solution.py:159
  (125 shorter events, 122.5 us)
Async XLA Ops:
  0.0 45.6 %copy-start = (bf16[512,512]{1,0:T(8,128)(2,1)S(1)}, bf16[512,512]{1,0:T(8,128)(2,1)}, u32[]{:S(2)}) copy-start(bf16[512,512]{1,0:T(8,128)(2,1)} %param.17) | copy-start | bytes 1572868
  0.0 9.2 %copy-start.9 = (f32[27,512]{1,0:T(8,128)S(1)}, f32[27,512]{1,0:T(8,128)}, u32[]{:S(2)}) copy-start(f32[27,512]{1,0:T(8,128)} %param.14) | copy-start | bytes 165892
  0.0 9.3 %copy-start.10 = (bf16[1024,512]{1,0:T(8,128)(2,1)S(1)}, bf16[1024,512]{1,0:T(8,128)(2,1)}, u32[]{:S(2)}) copy-start(bf16[1024,512]{1,0:T(8,128)(2,1)} %param.15) | copy-start | bytes 3145732
  0.0 9.3 %copy-start.11 = (bf16[512,512]{1,0:T(8,128)(2,1)S(1)}, bf16[512,512]{1,0:T(8,128)(2,1)}, u32[]{:S(2)}) copy-start(bf16[512,512]{1,0:T(8,128)(2,1)} %param.16) | copy-start | bytes 1572868
  2.9 26.2 %copy-start.4 = (bf16[8,16,16,512]{3,2,1,0:T(8,128)(2,1)}, bf16[8,16,16,512]{3,2,1,0:T(8,128)(2,1)S(1)}, u32[]{:S(2)}) copy-start(bf16[8,16,16,512]{3,2,1,0:T(8,128)(2,1)S(1)} %broadcast_multiply_fusion) | copy-start | bytes 6291460
  3.0 16.1 %collective-permute-start = (bf16[1,16,16,512]{3,2,1,0:T(8,128)(2,1)S(1)}, bf16[1,16,16,512]{3,2,1,0:T(8,128)(2,1)S(1)}, u32[]{:S(2)}, u32[]{:S(2)}) collective-permute-start(bf16[1,16,16,512]{3,2,1,0:T(8,128)(2,1)S(1)} %get-tuple-element.11), channel_id=1, source_target_pairs={{0,4},{4,8},{8,12},{12,16},{16,20},{20,24},{24,28},{1,5},{5,9},{9,... | collective-permute-start | bytes 786440 | tf_op jit(solution)/shard_map/ppermute | solution.py:18
  7.9 11.2 %collective-permute-start.1 = (bf16[1,16,16,512]{3,2,1,0:T(8,128)(2,1)S(1)}, bf16[1,16,16,512]{3,2,1,0:T(8,128)(2,1)S(1)}, u32[]{:S(2)}, u32[]{:S(2)}) collective-permute-start(bf16[1,16,16,512]{3,2,1,0:T(8,128)(2,1)S(1)} %get-tuple-element.12), channel_id=1, source_target_pairs={{4,0},{8,4},{12,8},{16,12},{20,16},{24,20},{28,24},{5,1},{9,5},{13... | collective-permute-start | bytes 786440 | tf_op jit(solution)/shard_map/ppermute | solution.py:20
  19.1 2.6 collective-permute-start.2
  20.4 5.0 %collective-permute-start.3 = (bf16[10,1,16,512]{3,2,1,0:T(8,128)(2,1)S(1)}, bf16[10,1,16,512]{3,2,1,0:T(8,128)(2,1)S(1)}, u32[]{:S(2)}, u32[]{:S(2)}) collective-permute-start(bf16[10,1,16,512]{3,2,1,0:T(8,128)(2,1)S(1)} %get-tuple-element.10), channel_id=1, source_target_pairs={{1,0},{2,1},{3,2},{5,4},{6,5},{7,6},{9,8},{10,9},{11,10},{13,12},{... | collective-permute-start | bytes 491528 | tf_op jit(solution)/shard_map/ppermute | solution.py:20
  45.5 24.7 %copy-start.6 = (bf16[8,16,16,512]{3,2,1,0:T(8,128)(2,1)}, bf16[8,16,16,512]{3,2,1,0:T(8,128)(2,1)S(1)}, u32[]{:S(2)}) copy-start(bf16[8,16,16,512]{3,2,1,0:T(8,128)(2,1)S(1)} %add_convert_fusion) | copy-start | bytes 6291460
  48.2 92.0 %copy-start.2 = (f32[1024,2048]{1,0:T(8,128)}, f32[1024,2048]{1,0:T(8,128)S(1)}, u32[]{:S(2)}) copy-start(f32[1024,2048]{1,0:T(8,128)S(1)} %get-tuple-element.55) | copy-start | bytes 25165828
  49.6 92.5 %copy-start.3 = (f32[1024,2048]{1,0:T(8,128)}, f32[1024,2048]{1,0:T(8,128)S(1)}, u32[]{:S(2)}) copy-start(f32[1024,2048]{1,0:T(8,128)S(1)} %get-tuple-element.53) | copy-start | bytes 25165828
  65.8 4.5 %copy-start.12 = (bf16[512,512]{1,0:T(8,128)(2,1)S(1)}, bf16[512,512]{1,0:T(8,128)(2,1)}, u32[]{:S(2)}) copy-start(bf16[512,512]{1,0:T(8,128)(2,1)} %param.18) | copy-start | bytes 1572868
  147.8 20.8 %all-to-all-start.1 = ((f32[32,1,256]{2,1,0:T(1,128)}), f32[32,1,256]{2,1,0:T(1,128)S(1)}, u32[]{:S(2)}, u32[]{:S(2)}) async-start(f32[32,1,256]{2,1,0:T(1,128)} %reshape.112), calls=%async_computation.1 | async-start | bytes 65536 | tf_op jit(solution)/shard_map/all_to_all | solution.py:121
  168.6 17.8 %all-to-all-start.2 = ((f32[32,1,256]{2,1,0:T(1,128)}), f32[32,1,256]{2,1,0:T(1,128)S(1)}, u32[]{:S(2)}, u32[]{:S(2)}) async-start(f32[32,1,256]{2,1,0:T(1,128)} %reshape.114), calls=%async_computation.2 | async-start | bytes 65536 | tf_op jit(solution)/shard_map/all_to_all | solution.py:120
  186.4 54.7 %all-to-all-start = ((f32[1,1024,512]{2,0,1:T(1,128)}), f32[1,1024,512]{2,0,1:T(1,128)}, u32[]{:S(2)}, u32[]{:S(2)}) async-start(f32[1,1024,512]{2,0,1:T(1,128)} %copy.23), calls=%async_computation | async-start | bytes 4194304 | tf_op jit(solution)/shard_map/all_to_all | solution.py:119
  202.9 40.4 %copy-start.8 = (bf16[512,512]{1,0:T(8,128)(2,1)S(1)}, bf16[512,512]{1,0:T(8,128)(2,1)}, u32[]{:S(2)}) copy-start(bf16[512,512]{1,0:T(8,128)(2,1)} %param.19) | copy-start | bytes 1572868
  242.8 20.0 %copy-start.13 = (bf16[512,512]{1,0:T(8,128)(2,1)S(1)}, bf16[512,512]{1,0:T(8,128)(2,1)}, u32[]{:S(2)}) copy-start(bf16[512,512]{1,0:T(8,128)(2,1)} %param.20) | copy-start | bytes 1572868
  244.3 1.2 collective-permute-start.4
  245.5 4.3 %collective-permute-start.5 = (bf16[64,512]{1,0:T(8,128)(2,1)S(1)}, bf16[64,512]{1,0:T(8,128)(2,1)S(1)}, u32[]{:S(2)}, u32[]{:S(2)}) collective-permute-start(bf16[64,512]{1,0:T(8,128)(2,1)S(1)} %maximum_select_fusion.6), channel_id=1, source_target_pairs={{0,2},{1,3},{2,0},{3,1},{4,6},{5,7},{6,4},{7,5},{8,10},{9,11},{10,... | collective-permute-start | bytes 196616 | tf_op jit(solution)/shard_map/ppermute | solution.py:139
  249.9 5.0 %collective-permute-start.6 = (bf16[128,512]{1,0:T(8,128)(2,1)S(1)}, bf16[128,512]{1,0:T(8,128)(2,1)S(1)}, u32[]{:S(2)}, u32[]{:S(2)}) collective-permute-start(bf16[128,512]{1,0:T(8,128)(2,1)S(1)} %maximum_select_fusion.5), channel_id=1, source_target_pairs={{0,4},{1,5},{2,6},{3,7},{4,0},{5,1},{6,2},{7,3},{8,12},{9,13},{10,... | collective-permute-start | bytes 393224 | tf_op jit(solution)/shard_map/ppermute | solution.py:139
  255.0 6.4 %collective-permute-start.7 = (bf16[256,512]{1,0:T(8,128)(2,1)S(1)}, bf16[256,512]{1,0:T(8,128)(2,1)S(1)}, u32[]{:S(2)}, u32[]{:S(2)}) collective-permute-start(bf16[256,512]{1,0:T(8,128)(2,1)S(1)} %maximum_select_fusion.2), channel_id=1, source_target_pairs={{0,8},{1,9},{2,10},{3,11},{4,12},{5,13},{6,14},{7,15},{8,0},{9,1},... | collective-permute-start | bytes 786440 | tf_op jit(solution)/shard_map/ppermute | solution.py:139
  261.6 22.7 %collective-permute-start.8 = (bf16[512,512]{1,0:T(8,128)(2,1)S(1)}, bf16[512,512]{1,0:T(8,128)(2,1)S(1)}, u32[]{:S(2)}, u32[]{:S(2)}) collective-permute-start(bf16[512,512]{1,0:T(8,128)(2,1)S(1)} %maximum_select_fusion.1), channel_id=1, source_target_pairs={{0,16},{1,17},{2,18},{3,19},{4,20},{5,21},{6,22},{7,23},{8,24},{9,... | collective-permute-start | bytes 1572872 | tf_op jit(solution)/shard_map/ppermute | solution.py:139
  262.8 21.5 %copy-start.14 = (bf16[512,512]{1,0:T(8,128)(2,1)S(1)}, bf16[512,512]{1,0:T(8,128)(2,1)}, u32[]{:S(2)}) copy-start(bf16[512,512]{1,0:T(8,128)(2,1)} %param.21) | copy-start | bytes 1572868
  335.5 5.0 %copy-start.15 = (bf16[512,512]{1,0:T(8,128)(2,1)S(1)}, bf16[512,512]{1,0:T(8,128)(2,1)}, u32[]{:S(2)}) copy-start(bf16[512,512]{1,0:T(8,128)(2,1)} %param.22) | copy-start | bytes 1572868
  351.1 10.2 %slice-start = ((s8[8388608]{0:T(1024)(128)(4,1)}), s8[4194304]{0:T(1024)(128)(4,1)S(1)}, s32[]{:S(2)}) async-start(s8[8388608]{0:T(1024)(128)(4,1)} %bitcast.72), calls=%async_computation.3 | async-start | bytes 8388608
  356.2 5.1 %slice-start.1 = ((s8[8388608]{0:T(1024)(128)(4,1)}), s8[4194304]{0:T(1024)(128)(4,1)S(1)}, s32[]{:S(2)}) async-start(s8[8388608]{0:T(1024)(128)(4,1)} %bitcast.72), calls=%async_computation.4 | async-start | bytes 8388608
  366.0 1.6 copy-start.5
  366.0 1.7 copy-start.7
  366.0 5.0 %copy-start.1 = (bf16[512,512]{1,0:T(8,128)(2,1)S(1)}, bf16[512,512]{1,0:T(8,128)(2,1)}, u32[]{:S(2)}) copy-start(bf16[512,512]{1,0:T(8,128)(2,1)} %param.17) | copy-start | bytes 1572868
